TPU v7x, 32 devices: a whole 2x2x4 slice. The times are simulated.
32 devices in a mesh: dp: 8 (over z, x), tensor: 4 (over y, core).
Axes of the slice: x: 2, y: 2, z: 4, core: 2. Of those that a mesh axis runs over, the one named last changes fastest.
Arguments:
- cells_x: bfloat16 [16384, 768], P(('dp', 'tensor')), may hold values from -6 to 6
- cotangent: bfloat16 [16384, 768], P(('dp', 'tensor')), may hold values from -6 to 6
- gene_counts: int32 [8], replicated, may hold values from 300 to 2048, as said below
- slot_cell: int32 [8], P('dp'), may hold values from 0 to 7, each once
- norm_gain: bfloat16 [2, 768], replicated, may hold values from 0.5 to 1.5
- norm_shift: bfloat16 [2, 768], replicated, may hold values from -1 to 1
- out_bias: bfloat16 [2, 768], replicated, may hold values from -1 to 1
- w_qkv: bfloat16 [3, 768, 768], P(None, None, 'tensor'), may hold values from -0.3125 to 0.3125
- qv_bias: bfloat16 [2, 768], P(None, 'tensor'), may hold values from -1.5 to 1.5
- w_out: bfloat16 [768, 768], P('tensor'), may hold values from -1.75 to 1.75
- w_up: bfloat16 [768, 3072], P(None, 'tensor'), may hold values from -0.21875 to 0.21875
- up_bias: bfloat16 [3072], P('tensor'), may hold values from -1.5 to 1.5
- w_down: bfloat16 [3072, 768], P('tensor'), may hold values from -0.109375 to 0.109375
Outputs:
- block_out: bfloat16 [16384, 768], P(('dp', 'tensor'))
- input_grad: bfloat16 [16384, 768], P(('dp', 'tensor'))
- grad_norm_gain: float32 [2, 768], replicated
- grad_norm_shift: float32 [2, 768], replicated
- grad_out_bias: float32 [2, 768], replicated
- grad_qkv: float32 [3, 768, 768], P(None, None, 'tensor')
- grad_qv_bias: float32 [2, 768], P(None, 'tensor')
- grad_w_out: float32 [768, 768], P('tensor')
- grad_w_up: float32 [768, 3072], P(None, 'tensor')
- grad_up_bias: float32 [3072], P('tensor')
- grad_w_down: float32 [3072, 768], P('tensor')
Inputs may be any that keep to these rules, and one draw needn't show every extreme that they name: `gene_counts`: some cell has exactly 2048 expressed genes and some exactly 300. `slot_cell`: every cell is held in exactly one slot.
All inputs are finite; a program needn't handle non-finite values.
Results may differ from a plain program's by a relative error of at most 0.013.
The roundings to bfloat16 on the way count: a program that leaves them out, or rounds other values in their place, can miss the bound.
Values may be sent and summed in bfloat16 or wider, within the bound.
No kernel may reach another device: no remote copies, remote signals or barrier semaphores. Data moves between devices by JAX's collectives and lax.ppermute only.
A program may use at most 128 MiB of HBM per device.

v0:
```python
import jax
import jax.numpy as jnp
from jax import lax
from jax.sharding import PartitionSpec as P

HEAD_DIM = 64
SLOT = 2048


EPSILON = 1e-05
NEGATIVE = -1e30


def exact_gelu(hidden):
    return jax.nn.gelu(hidden, approximate=False)


def normalize(features, gain_row, shift_row):
    row_mean = jnp.mean(features, axis=-1, keepdims=True)
    centered = features - row_mean
    variance = jnp.mean(centered * centered, axis=-1, keepdims=True)
    inverse = lax.rsqrt(variance + EPSILON)
    scaled = centered * inverse
    return (scaled * gain_row.astype(jnp.float32) + shift_row.astype(jnp.float32), scaled, inverse)


def normalize_back(upstream, scaled, inverse, gain_row):
    graded = upstream * gain_row.astype(jnp.float32)
    grad_mean = jnp.mean(graded, axis=-1, keepdims=True)
    cross_mean = jnp.mean(graded * scaled, axis=-1, keepdims=True)
    return (
        inverse * (graded - grad_mean - scaled * cross_mean),
        jnp.sum(upstream * scaled, axis=0),
        jnp.sum(upstream, axis=0),
    )


def contract_last(left, right):
    return lax.dot_general(
        left, right, (((1,), (1,)), ((), ())), preferred_element_type=jnp.float32
    )


def contract_first(left, right):
    return lax.dot_general(
        left, right, (((0,), (0,)), ((), ())), preferred_element_type=jnp.float32
    )


def masked_scores(block_queries, key_heads, live_keys, score_scale):
    scores = (
        jnp.einsum("qhe,khe->hqk", block_queries, key_heads, preferred_element_type=jnp.float32)
        * score_scale
    )
    return jnp.where(live_keys[None, None, :], scores, NEGATIVE)


def attend_cell(query_heads, key_heads, value_heads, live_keys, block_rows):
    score_scale = query_heads.shape[-1] ** (-0.5)

    def one_block(block_index):
        block_queries = lax.dynamic_slice_in_dim(
            query_heads, block_index * block_rows, block_rows, 0
        )
        scores = masked_scores(block_queries, key_heads, live_keys, score_scale)
        row_max = jnp.max(scores, axis=-1, keepdims=True)
        exp_scores = jnp.exp(scores - row_max)
        row_total = jnp.sum(exp_scores, axis=-1, keepdims=True)
        soft_low = (exp_scores / row_total).astype(jnp.bfloat16)
        attended = jnp.einsum(
            "hqk,khe->qhe", soft_low, value_heads, preferred_element_type=jnp.float32
        )
        return (attended, (row_max + jnp.log(row_total))[..., 0])

    attended, log_totals = lax.map(one_block, jnp.arange(query_heads.shape[0] // block_rows))
    return (attended.reshape(query_heads.shape[0], -1), log_totals)


def attend_back(query_heads, key_heads, value_heads, grad_heads, log_totals, live_keys, block_rows):
    score_scale = query_heads.shape[-1] ** (-0.5)
    slot_rows = query_heads.shape[0]

    def one_block(sums_carry, block_index):
        key_sum, value_sum = sums_carry
        first_row = block_index * block_rows
        block_queries = lax.dynamic_slice_in_dim(query_heads, first_row, block_rows, 0)
        block_grads = lax.dynamic_slice_in_dim(grad_heads, first_row, block_rows, 0)
        scores = masked_scores(block_queries, key_heads, live_keys, score_scale)
        softmaxed = jnp.exp(scores - log_totals[block_index][..., None])
        soft_low = softmaxed.astype(jnp.bfloat16)
        prob_grad = jnp.einsum(
            "qhe,khe->hqk", block_grads, value_heads, preferred_element_type=jnp.float32
        )
        row_inner = jnp.sum(softmaxed * prob_grad, axis=-1, keepdims=True)
        score_grad = (score_scale * softmaxed * (prob_grad - row_inner)).astype(jnp.bfloat16)
        query_grad = jnp.einsum(
            "hqk,khe->qhe", score_grad, key_heads, preferred_element_type=jnp.float32
        )
        key_sum = key_sum + jnp.einsum(
            "hqk,qhe->khe", score_grad, block_queries, preferred_element_type=jnp.float32
        )
        value_sum = value_sum + jnp.einsum(
            "hqk,qhe->khe", soft_low, block_grads, preferred_element_type=jnp.float32
        )
        return ((key_sum, value_sum), query_grad)

    zero_heads = jnp.zeros(key_heads.shape, jnp.float32)
    (key_sum, value_sum), query_grad = lax.scan(
        one_block, (zero_heads, zero_heads), jnp.arange(slot_rows // block_rows)
    )
    return (
        query_grad.reshape(slot_rows, -1).astype(jnp.bfloat16),
        key_sum.reshape(slot_rows, -1).astype(jnp.bfloat16),
        value_sum.reshape(slot_rows, -1).astype(jnp.bfloat16),
    )


def per_device(
    cells_x,
    cotangent,
    gene_counts,
    slot_cell,
    norm_gain,
    norm_shift,
    out_bias,
    w_qkv,
    qv_bias,
    w_out,
    w_up,
    up_bias,
    w_down,
):
    row_count = cells_x.shape[0]
    cells_dev = slot_cell.shape[0]
    group_rows = cells_dev * SLOT
    block_rows = min(512, SLOT)
    cell_ids = jnp.arange(gene_counts.shape[0], dtype=jnp.int32)
    lengths = jnp.sum(
        jnp.where(slot_cell[:, None] == cell_ids[None, :], gene_counts[None, :], 0), axis=1
    )
    positions = jnp.arange(SLOT, dtype=jnp.int32)
    live_keys = positions[None, :] < lengths[:, None]
    row_index = lax.axis_index("tensor") * row_count + jnp.arange(row_count, dtype=jnp.int32)
    cell_of = row_index // SLOT
    length_of = jnp.sum(
        jnp.where(
            cell_of[:, None] == jnp.arange(cells_dev, dtype=jnp.int32)[None, :], lengths[None, :], 0
        ),
        axis=1,
    )
    live_rows = row_index % SLOT < length_of
    inputs = cells_x.astype(jnp.float32)
    normed_in, scaled_in, inverse_in = normalize(inputs, norm_gain[0], norm_shift[0])
    gathered_in = lax.all_gather(normed_in.astype(jnp.bfloat16), "tensor", axis=0, tiled=True)
    bias_rows = jnp.stack([qv_bias[0], jnp.zeros_like(qv_bias[0]), qv_bias[1]]).astype(jnp.float32)
    projected = jnp.einsum("rd,sdc->src", gathered_in, w_qkv, preferred_element_type=jnp.float32)
    projected = (projected + bias_rows[:, None, :]).astype(jnp.bfloat16)
    heads_local = projected.shape[2] // HEAD_DIM
    head_parts = projected.reshape(3, cells_dev, SLOT, heads_local, HEAD_DIM)
    attended, log_totals = lax.map(
        lambda packed: attend_cell(packed[0], packed[1], packed[2], packed[3], block_rows),
        (head_parts[0], head_parts[1], head_parts[2], live_keys),
    )
    attended_low = attended.reshape(group_rows, -1).astype(jnp.bfloat16)
    attn_sum = lax.psum_scatter(
        jnp.dot(attended_low, w_out, preferred_element_type=jnp.float32),
        "tensor",
        scatter_dimension=0,
        tiled=True,
    )
    middle = inputs + attn_sum + out_bias[0].astype(jnp.float32)
    normed_mid, scaled_mid, inverse_mid = normalize(middle, norm_gain[1], norm_shift[1])
    normed_mid_low = normed_mid.astype(jnp.bfloat16)
    up_full, bias_full, down_full = (w_up, up_bias, w_down)
    ffn_rows = lax.all_gather(normed_mid_low, "tensor", axis=0, tiled=True)
    hidden = jnp.dot(ffn_rows, up_full, preferred_element_type=jnp.float32) + bias_full.astype(
        jnp.float32
    )
    active, gelu_back = jax.vjp(exact_gelu, hidden)
    active_low = active.astype(jnp.bfloat16)
    branch = lax.psum_scatter(
        jnp.dot(active_low, w_down, preferred_element_type=jnp.float32).astype(jnp.bfloat16),
        "tensor",
        scatter_dimension=0,
        tiled=True,
    ).astype(jnp.float32)
    output = jnp.where(live_rows[:, None], middle + branch + out_bias[1].astype(jnp.float32), 0.0)
    block_out = output.astype(jnp.bfloat16)
    out_grad = jnp.where(live_rows[:, None], cotangent, jnp.zeros_like(cotangent))
    grad_rows = lax.all_gather(out_grad, "tensor", axis=0, tiled=True)
    hidden_grad = gelu_back(contract_last(grad_rows, down_full))[0].astype(jnp.bfloat16)
    down_grad = contract_first(active_low, grad_rows)
    up_grad = contract_first(ffn_rows, hidden_grad)
    up_bias_grad = jnp.sum(hidden_grad, axis=0, dtype=jnp.float32)
    mid_norm_grad = lax.psum_scatter(
        contract_last(hidden_grad, w_up), "tensor", scatter_dimension=0, tiled=True
    )
    mid_back, gain_mid, shift_mid = normalize_back(
        mid_norm_grad, scaled_mid, inverse_mid, norm_gain[1]
    )
    middle_grad = out_grad.astype(jnp.float32) + mid_back
    middle_rows = lax.all_gather(middle_grad.astype(jnp.bfloat16), "tensor", axis=0, tiled=True)
    attended_grad = contract_last(middle_rows, w_out).astype(jnp.bfloat16)
    out_weight_grad = contract_first(attended_low, middle_rows)
    grad_heads = attended_grad.reshape(cells_dev, SLOT, heads_local, HEAD_DIM)
    query_grad, key_grad, value_grad = lax.map(
        lambda packed: attend_back(
            packed[0], packed[1], packed[2], packed[3], packed[4], packed[5], block_rows
        ),
        (head_parts[0], head_parts[1], head_parts[2], grad_heads, log_totals, live_keys),
    )
    qkv_grad = jnp.stack([query_grad, key_grad, value_grad]).reshape(3, group_rows, -1)
    qkv_weight_grad = jnp.einsum(
        "src,rd->sdc", qkv_grad, gathered_in, preferred_element_type=jnp.float32
    )
    qv_bias_grad = jnp.stack(
        [
            jnp.sum(qkv_grad[0], axis=0, dtype=jnp.float32),
            jnp.sum(qkv_grad[2], axis=0, dtype=jnp.float32),
        ]
    )
    in_norm_grad = lax.psum_scatter(
        jnp.einsum("src,sdc->rd", qkv_grad, w_qkv, preferred_element_type=jnp.float32),
        "tensor",
        scatter_dimension=0,
        tiled=True,
    )
    in_back, gain_in, shift_in = normalize_back(in_norm_grad, scaled_in, inverse_in, norm_gain[0])
    input_grad = (middle_grad + in_back).astype(jnp.bfloat16)
    gain_grad, shift_grad, bias_grad = lax.psum(
        (
            jnp.stack([gain_in, gain_mid]),
            jnp.stack([shift_in, shift_mid]),
            jnp.stack([jnp.sum(middle_grad, axis=0), jnp.sum(out_grad, axis=0, dtype=jnp.float32)]),
        ),
        "tensor",
    )
    (
        qkv_weight_grad,
        qv_bias_grad,
        out_weight_grad,
        up_grad,
        up_bias_grad,
        down_grad,
        gain_grad,
        shift_grad,
        bias_grad,
    ) = lax.psum(
        (
            qkv_weight_grad,
            qv_bias_grad,
            out_weight_grad,
            up_grad,
            up_bias_grad,
            down_grad,
            gain_grad,
            shift_grad,
            bias_grad,
        ),
        "dp",
    )
    return (
        block_out,
        input_grad,
        gain_grad,
        shift_grad,
        bias_grad,
        qkv_weight_grad,
        qv_bias_grad,
        out_weight_grad,
        up_grad,
        up_bias_grad,
        down_grad,
    )


def solution(mesh):
    return jax.shard_map(
        per_device,
        mesh=mesh,
        in_specs=(
            P(("dp", "tensor"), None),
            P(("dp", "tensor"), None),
            P(),
            P("dp"),
            P(),
            P(),
            P(),
            P(None, None, "tensor"),
            P(None, "tensor"),
            P("tensor", None),
            P(None, "tensor"),
            P("tensor"),
            P("tensor", None),
        ),
        out_specs=(
            P(("dp", "tensor"), None),
            P(("dp", "tensor"), None),
            P(),
            P(),
            P(),
            P(None, None, "tensor"),
            P(None, "tensor"),
            P("tensor", None),
            P(None, "tensor"),
            P("tensor"),
            P("tensor", None),
        ),
        check_vma=False,
    )
```

profile of v0, /device:TPU:0, one launch (start us, length us, event | category | flops | bytes accessed | tf_op | source)
XLA Modules:
  0.0 833.2 jit_solution(6018540514751062280)
XLA Ops:
  15.0 29.9 %all-gather.5.cloned.1.call-done = bf16[2048,768]{1,0:T(8,128)(2,1)} async-done(((bf16[512,768]{1,0:T(8,128)(2,1)}), bf16[2048,768]{1,0:T(8,128)(2,1)}) %all-gather.5.cloned.1.call-update) | async-done | bytes 3145744 | tf_op jit(solution)/shard_map/all_gather | solution.py:154
  50.3 45.2 %while.48 = (s32[]{:T(128)}, bf16[4,512,3,64]{1,3,2,0:T(8,128)(2,1)}, f32[4,3,512]{2,1,0:T(4,128)}, s32[4]{0:T(128)S(1)}, bf16[2048,3,64]{0,2,1:T(8,128)(2,1)S(1...) while((s32[]{:T(128)}, ...), condition=%wide.region_6.7_spmd.clone, body=%wide.region_3.6_spmd.clone.sunk | while | flops 843055616 | bytes 46266624 | solution.py:75
  103.9 57.7 %reduce-scatter.5.cloned.1.call-done = f32[512,768]{1,0:T(8,128)} async-done(((f32[2048,768]{1,0:T(8,128)}), f32[512,768]{1,0:T(8,128)}) %reduce-scatter.5.cloned.1.call-update) | async-done | bytes 1572880 | tf_op jit(solution)/shard_map/reduce_scatter | solution.py:165
  170.1 23.7 %all-gather.7.cloned.1.call-done = bf16[2048,768]{1,0:T(8,128)(2,1)} async-done(((bf16[512,768]{1,0:T(8,128)(2,1)}), bf16[2048,768]{1,0:T(8,128)(2,1)}) %all-gather.7.cloned.1.call-update) | async-done | bytes 3145744 | tf_op jit(solution)/shard_map/all_gather | solution.py:175
  193.8 7.5 fusion.75
  201.3 23.0 %all-gather.9.cloned.1.call-done = bf16[2048,768]{1,0:T(8,128)(2,1)} async-done(((bf16[512,768]{1,0:T(8,128)(2,1)}), bf16[2048,768]{1,0:T(8,128)(2,1)}) %all-gather.9.cloned.1.call-update) | async-done | bytes 3145744 | tf_op jit(solution)/shard_map/all_gather | solution.py:190
  224.3 20.2 %convert_reduce_fusion = (f32[768]{0:T(1024)}, bf16[2048,768]{1,0:T(8,128)(2,1)S(1)}, f32[2048,768]{1,0:T(8,128)}) fusion(f32[2048,768]{1,0:T(8,128)} %fusion.75, f32[768]{0:T(1024)S(1)} %convert_element_type.147, bf16[2048,768]{1,0:T(8,128)(2,1)} %all-gather.9.cloned.1.call-done, bf16[768,768]{1,0:T(8,128)(2,1)S(1)} %copy-done), kind=kOutput, calls=%fused_computation.45 | convolution fusion | flops 2533883136 | bytes 20060160 | tf_op jit(solution)/shard_map/dot_general | solution.py:39
  262.1 47.7 %reduce-scatter.9.cloned.1.call-done = f32[512,768]{1,0:T(8,128)} async-done(((f32[2048,768]{1,0:T(8,128)}), f32[512,768]{1,0:T(8,128)}) %reduce-scatter.9.cloned.1.call-update) | async-done | bytes 1572880 | tf_op jit(solution)/shard_map/reduce_scatter | solution.py:195
  312.5 37.6 %reduce-scatter.7.cloned.1.call-done = bf16[512,768]{1,0:T(8,128)(2,1)} async-done(((bf16[2048,768]{1,0:T(8,128)(2,1)}), bf16[512,768]{1,0:T(8,128)(2,1)}) %reduce-scatter.7.cloned.1.call-update) | async-done | bytes 786448 | tf_op jit(solution)/shard_map/reduce_scatter | solution.py:181
  356.2 28.4 %all-gather.11.cloned.1.call-done = bf16[2048,768]{1,0:T(8,128)(2,1)} async-done(((bf16[512,768]{1,0:T(8,128)(2,1)}), bf16[2048,768]{1,0:T(8,128)(2,1)}) %all-gather.11.cloned.1.call-update) | async-done | bytes 3145744 | tf_op jit(solution)/shard_map/all_gather | solution.py:202
  389.4 122.9 %while.49 = (s32[]{:T(128)}, f32[2048,3,64]{0,2,1:T(8,128)S(1)}, f32[2048,3,64]{0,2,1:T(8,128)}, bf16[4,512,3,64]{1,3,2,0:T(8,128)(2,1)}, s32[4]{0:T(128)S(1)}, ...) while((s32[]{:T(128)}, f32[2048,3,64]{0,2,1:T(8,128)S(1)}, ...), condition=%wide.region_16.17_spmd.clone, body=%wide.region_14.16_spmd.clone.sunk | while | flops 2065170944 | bytes 129419576 | solution.py:108
  411.7 5.6 fusion.146
  426.9 5.5 fusion.145
  442.5 5.6 fusion.146
  457.7 5.5 fusion.145
  473.4 5.6 fusion.146
  488.6 5.5 fusion.145
  504.3 5.6 fusion.146
  516.6 6.0 convolution_bitcast_fusion.2
  522.8 7.1 fusion.78
  543.3 38.4 %reduce-scatter.11.cloned.1.call-done = f32[512,768]{1,0:T(8,128)} async-done(((f32[2048,768]{1,0:T(8,128)}), f32[512,768]{1,0:T(8,128)}) %reduce-scatter.11.cloned.1.call-update) | async-done | bytes 1572880 | tf_op jit(solution)/shard_map/reduce_scatter | solution.py:222
  583.9 10.2 %all-reduce.2 = (f32[2,768]{1,0:T(2,128)S(1)}, f32[2,768]{1,0:T(2,128)S(1)}, f32[2,768]{1,0:T(2,128)S(1)}) all-reduce(f32[2,768]{1,0:T(2,128)S(1)} %pad_maximum_fusion.1, f32[2,768]{1,0:T(2,128)S(1)} %pad_maximum_fusion.2, f32[2,768]{1,0:T(2,128)S(1)} %pad_maximum_fusion.3), channel_id=1, replica_groups=mesh['dp'=8,'tensor'=4] {'tensor'}, use_global_device_ids=true, to_apply=%region_22.23 | all-reduce | flops 4608 | bytes 36864 | tf_op jit(solution)/shard_map/psum | solution.py:230
  594.2 40.2 %all-reduce = (f32[2,768]{1,0:T(2,128)}, f32[2,768]{1,0:T(2,128)}, f32[2,768]{1,0:T(2,128)}, f32[2,192]{1,0:T(2,128)}, f32[768]{0:T(1024)}) all-reduce(f32[2,768]{1,0:T(2,128)S(1)} %get-tuple-element.288, f32[2,768]{1,0:T(2,128)S(1)} %get-tuple-element.289, ...), channel_id=1, replica_groups=mesh['dp'=8,'tensor'=4] {'dp'}, use_global_device_ids=true, to_apply=%region_23.24 | all-reduce | flops 5760 | bytes 46080 | tf_op jit(solution)/shard_map/psum | solution.py:248
  637.2 182.5 %all-reduce.5.cloned.1.call-done = (f32[3,768,192]{1,2,0:T(8,128)}, f32[192,768]{1,0:T(8,128)}, f32[768,768]{1,0:T(8,128)}, f32[768,768]{1,0:T(8,128)}) async-done(((f32[3,768,192]{1,2,0:T(8,128)}, f32[192,768]{1,0:T(8,128)}, f32[768,768]{1,0:T(8,128)}, f32[768,768]{1,0:T(8,128)}), (f32[3,768,192]{1,2,0:T(8,128)}, f32[192,768]{1,0:T(8,128)}, f32[768,768]{1,0:T(8,128)}, ...) | async-done | bytes 7077904 | tf_op jit(solution)/shard_map/psum | solution.py:248
  (253 shorter events, 206.0 us)
Async XLA Ops:
  7.2 217.1 %copy-start = (bf16[768,768]{1,0:T(8,128)(2,1)S(1)}, bf16[768,768]{1,0:T(8,128)(2,1)}, u32[]{:S(2)}) copy-start(bf16[768,768]{1,0:T(8,128)(2,1)} %param.29) | copy-start | bytes 3538948
  7.2 37.6 %copy-start.44 = (bf16[3,768,192]{1,2,0:T(8,128)(2,1)S(1)}, bf16[3,768,192]{1,2,0:T(8,128)(2,1)}, u32[]{:S(2)}) copy-start(bf16[3,768,192]{1,2,0:T(8,128)(2,1)} %param.24) | copy-start | bytes 2654212
  7.2 37.6 %all-gather.5.cloned.1.call-start = ((), (), s32[]{:S(2)}) async-start(), calls=%async_computation.4 | async-start | bytes 3932160 | tf_op jit(solution)/shard_map/all_gather | solution.py:154
  8.7 40.1 %copy-start.27 = (f32[512]{0:T(512)}, f32[512]{0:T(512)S(1)}, u32[]{:S(2)}) copy-start(f32[512]{0:T(512)S(1)} %broadcast_multiply_fusion.5) | copy-start | bytes 6148
  10.2 38.5 %copy-start.29 = (f32[512]{0:T(512)}, f32[512]{0:T(512)S(1)}, u32[]{:S(2)}) copy-start(f32[512]{0:T(512)S(1)} %add_rsqrt_fusion.1) | copy-start | bytes 6148
  11.1 37.7 %copy-start.25 = (f32[768]{0:T(1024)}, f32[768]{0:T(1024)S(1)}, u32[]{:S(2)}) copy-start(f32[768]{0:T(1024)S(1)} %get-tuple-element.312) | copy-start | bytes 9220
  13.5 148.2 %reduce-scatter.5.cloned.1.call-start = ((), (), s32[]{:S(2)}) async-start(), calls=%async_computation.5 | async-start | bytes 7864320 | tf_op jit(solution)/shard_map/reduce_scatter | solution.py:165
  102.7 91.1 %all-gather.7.cloned.1.call-start = ((), (), s32[]{:S(2)}) async-start(), calls=%async_computation.6 | async-start | bytes 3932160 | tf_op jit(solution)/shard_map/all_gather | solution.py:175
  165.1 59.2 %all-gather.9.cloned.1.call-start = ((), (), s32[]{:S(2)}) async-start(), calls=%async_computation.8 | async-start | bytes 3932160 | tf_op jit(solution)/shard_map/all_gather | solution.py:190
  169.2 140.6 %reduce-scatter.9.cloned.1.call-start = ((), (), s32[]{:S(2)}) async-start(), calls=%async_computation.9 | async-start | bytes 7864320 | tf_op jit(solution)/shard_map/reduce_scatter | solution.py:195
  250.8 99.3 %reduce-scatter.7.cloned.1.call-start = ((), (), s32[]{:S(2)}) async-start(), calls=%async_computation.7 | async-start | bytes 3932160 | tf_op jit(solution)/shard_map/reduce_scatter | solution.py:181
  262.0 88.1 %copy-start.11 = (bf16[512,768]{1,0:T(8,128)(2,1)S(1)}, bf16[512,768]{1,0:T(8,128)(2,1)}, u32[]{:S(2)}) copy-start(bf16[512,768]{1,0:T(8,128)(2,1)} %get-tuple-element.299) | copy-start | bytes 2359300
  262.1 88.1 %copy-start.31 = (f32[768]{0:T(1024)S(1)}, f32[768]{0:T(1024)}, u32[]{:S(2)}) copy-start(f32[768]{0:T(1024)} %get-tuple-element.235) | copy-start | bytes 9220
  262.1 88.1 %copy-start.40 = (pred[512]{0:T(512)(128)(4,1)S(1)}, pred[512]{0:T(512)(128)(4,1)}, u32[]{:S(2)}) copy-start(pred[512]{0:T(512)(128)(4,1)} %copy-done.39) | copy-start | bytes 1540
  262.1 122.5 %all-gather.11.cloned.1.call-start = ((), (), s32[]{:S(2)}) async-start(), calls=%async_computation.10 | async-start | bytes 3932160 | tf_op jit(solution)/shard_map/all_gather | solution.py:202
  355.9 225.8 %reduce-scatter.11.cloned.1.call-start = ((), (), s32[]{:S(2)}) async-start(), calls=%async_computation.11 | async-start | bytes 7864320 | tf_op jit(solution)/shard_map/reduce_scatter | solution.py:222
  356.2 33.3 %copy-start.4 = (bf16[2048,3,64]{0,2,1:T(8,128)(2,1)S(1)}, bf16[2048,3,64]{0,2,1:T(8,128)(2,1)}, u32[]{:S(2)}) copy-start(bf16[2048,3,64]{0,2,1:T(8,128)(2,1)} %copy-done.3) | copy-start | bytes 2359300
  522.7 297.0 %all-reduce.5.cloned.1.call-start = ((), (), s32[]{:S(2)}) async-start(), calls=%async_computation.12 | async-start | bytes 14155776 | tf_op jit(solution)/shard_map/psum | solution.py:248
  541.8 39.9 %copy-start.5 = (bf16[512,768]{1,0:T(8,128)(2,1)S(1)}, bf16[512,768]{1,0:T(8,128)(2,1)}, u32[]{:S(2)}) copy-start(bf16[512,768]{1,0:T(8,128)(2,1)} %param.17) | copy-start | bytes 2359300
  541.8 39.9 %copy-start.26 = (f32[768]{0:T(1024)S(1)}, f32[768]{0:T(1024)}, u32[]{:S(2)}) copy-start(f32[768]{0:T(1024)} %copy-done.25) | copy-start | bytes 9220
  541.8 39.9 %copy-start.28 = (f32[512]{0:T(512)S(1)}, f32[512]{0:T(512)}, u32[]{:S(2)}) copy-start(f32[512]{0:T(512)} %copy-done.27) | copy-start | bytes 6148
  541.8 39.9 %copy-start.30 = (f32[512]{0:T(512)S(1)}, f32[512]{0:T(512)}, u32[]{:S(2)}) copy-start(f32[512]{0:T(512)} %copy-done.29) | copy-start | bytes 6148
  541.9 52.3 %copy-start.38 = (f32[768]{0:T(1024)S(1)}, f32[768]{0:T(1024)}, u32[]{:S(2)}) copy-start(f32[768]{0:T(1024)} %get-tuple-element.291) | copy-start | bytes 9220
  541.9 92.5 %copy-start.8 = (f32[512,768]{1,0:T(8,128)S(1)}, f32[512,768]{1,0:T(8,128)}, u32[]{:S(2)}) copy-start(f32[512,768]{1,0:T(8,128)} %copy-done.7) | copy-start | bytes 4718596
  (41 other events, 179.4 us)
Sparse Core Ops, SparseCore 0:
  13.6 31.2 all-gather.4
  102.8 58.8 reduce-scatter.4
  165.2 28.4 all-gather.6
  195.8 28.4 all-gather.8
  251.0 58.8 reduce-scatter.8
  312.2 37.8 reduce-scatter.6
  356.0 28.4 all-gather.10
  522.8 58.8 reduce-scatter.10
  587.3 232.3 all-reduce.4
where the time goes:
time: 842 us; the launch traced here: 833 us
  waiting for transfers between devices  469 us (56%)
  matrix products  177 us (21%)
  other arithmetic  75.6 us (9%)
  blocking collectives  50.4 us (6%)
  local copies, waits for them, and re-layouts  33 us (4%)
  between operations  15.4 us (2%)
  loops' own time  12.7 us (2%)
    psum x1, waiting for transfers between devices, per_device(): lax.psum((qkv_weight_grad, qv_bias_grad, out_weight_grad, up_grad, up_bia...  182 us
    reduce_scatter x1, waiting for transfers between devices, per_device(): lax.psum_scatter(jnp.dot(attended_low, w_out, preferred_element_type=jnp....  57.7 us
    reduce_scatter x1, waiting for transfers between devices, per_device(): lax.psum_scatter(contract_last(hidden_grad, w_up), 'tensor', scatter_dime...  47.7 us
    psum x1, blocking collectives, per_device(): lax.psum((qkv_weight_grad, qv_bias_grad, out_weight_grad, up_grad, up_bia...  40.2 us
    reduce_scatter x1, waiting for transfers between devices, per_device(): lax.psum_scatter(jnp.einsum('src,sdc->rd', qkv_grad, w_qkv, preferred_ele...  38.4 us
    reduce_scatter x1, waiting for transfers between devices, per_device(): lax.psum_scatter(jnp.dot(active_low, w_down, preferred_element_type=jnp.f...  37.6 us
    all_gather x1, waiting for transfers between devices, per_device(): lax.all_gather(normed_in.astype(jnp.bfloat16), 'tensor', axis=0, tiled=True)  29.9 us
    dot_general x3, matrix products, contract_last(): lax.dot_general(left, right, (((1,), (1,)), ((), ())), preferred_element_...  28.7 us
  transfers between devices with their start and end apart: 9, of which 9 were waited for; matrix products, arithmetic and copies ran while one was open for 6% of the time, Pallas kernels for 0%

commit v1 on v0

--- a/solution.py
+++ b/solution.py
@@ -113,6 +113,61 @@
         key_sum.reshape(slot_rows, -1).astype(jnp.bfloat16),
         value_sum.reshape(slot_rows, -1).astype(jnp.bfloat16),
     )
+
+
+def pair_swap(array, axis, bit):
+    size = lax.axis_size(axis)
+    return lax.ppermute(array, axis, [(source, source ^ bit) for source in range(size)])
+
+
+def gather_relative(rows):
+    across = pair_swap(rows, "tensor", 2)
+    beside = pair_swap(rows, "tensor", 1)
+    return (rows, beside, across, pair_swap(across, "tensor", 1))
+
+
+def scatter_relative(blocks):
+    low = [block.astype(jnp.bfloat16) for block in blocks]
+    far = blocks[2] + pair_swap(low[3], "tensor", 1).astype(jnp.float32)
+    far_low = pair_swap(far.astype(jnp.bfloat16), "tensor", 2)
+    near = blocks[0] + pair_swap(low[1], "tensor", 1).astype(jnp.float32)
+    return near + far_low.astype(jnp.float32)
+
+
+def reduce_cells(grads, bits):
+    index = lax.axis_index("dp")
+    block = grads
+    for bit in bits:
+        half = block.shape[0] // 2
+        side = (index // bit) % 2
+        kept = lax.dynamic_slice_in_dim(block, side * half, half, 0)
+        sent = lax.dynamic_slice_in_dim(block, (1 - side) * half, half, 0)
+        got = pair_swap(sent.astype(jnp.bfloat16), "dp", bit)
+        block = kept + got.astype(jnp.float32)
+    block = block.astype(jnp.bfloat16)
+    for bit in reversed(bits):
+        side = (index // bit) % 2
+        got = pair_swap(block, "dp", bit)
+        block = jnp.where(
+            side == 0, jnp.concatenate([block, got]), jnp.concatenate([got, block])
+        )
+    return block.astype(jnp.float32)
+
+
+def sum_cells(grads):
+    bits = [1 << step for step in range((lax.axis_size("dp") - 1).bit_length())]
+    half = grads.shape[0] // 2
+    rotated = bits[1:] + bits[:1]
+    return jnp.concatenate([reduce_cells(grads[:half], bits), reduce_cells(grads[half:], rotated)])
+
+
+def sum_small(rows, axes):
+    for axis in axes:
+        bit = 1
+        while bit < lax.axis_size(axis):
+            rows = rows + pair_swap(rows, axis, bit)
+            bit *= 2
+    return rows
 
 
 def per_device(
@@ -130,146 +185,109 @@
     up_bias,
     w_down,
 ):
-    row_count = cells_x.shape[0]
-    cells_dev = slot_cell.shape[0]
-    group_rows = cells_dev * SLOT
-    block_rows = min(512, SLOT)
+    rows = cells_x.shape[0]
+    width = cells_x.shape[1]
+    place = lax.axis_index("tensor")
     cell_ids = jnp.arange(gene_counts.shape[0], dtype=jnp.int32)
-    lengths = jnp.sum(
-        jnp.where(slot_cell[:, None] == cell_ids[None, :], gene_counts[None, :], 0), axis=1
-    )
-    positions = jnp.arange(SLOT, dtype=jnp.int32)
-    live_keys = positions[None, :] < lengths[:, None]
-    row_index = lax.axis_index("tensor") * row_count + jnp.arange(row_count, dtype=jnp.int32)
-    cell_of = row_index // SLOT
-    length_of = jnp.sum(
-        jnp.where(
-            cell_of[:, None] == jnp.arange(cells_dev, dtype=jnp.int32)[None, :], lengths[None, :], 0
-        ),
-        axis=1,
-    )
-    live_rows = row_index % SLOT < length_of
-    inputs = cells_x.astype(jnp.float32)
-    normed_in, scaled_in, inverse_in = normalize(inputs, norm_gain[0], norm_shift[0])
-    gathered_in = lax.all_gather(normed_in.astype(jnp.bfloat16), "tensor", axis=0, tiled=True)
+    length = jnp.sum(jnp.where(slot_cell[0] == cell_ids, gene_counts, 0))
+    positions = jnp.concatenate(
+        [(place ^ block) * rows + jnp.arange(rows, dtype=jnp.int32) for block in range(4)]
+    )
+    live_keys = positions < length
+    live_rows = live_keys[:rows]
+    x_rows = jnp.concatenate(gather_relative(cells_x))
+    out_grad = jnp.where(live_rows[:, None], cotangent, jnp.zeros_like(cotangent))
+    grad_rows = jnp.concatenate(gather_relative(out_grad))
+    normed_in, scaled_in, inverse_in = normalize(
+        x_rows.astype(jnp.float32), norm_gain[0], norm_shift[0]
+    )
+    gathered_in = normed_in.astype(jnp.bfloat16)
     bias_rows = jnp.stack([qv_bias[0], jnp.zeros_like(qv_bias[0]), qv_bias[1]]).astype(jnp.float32)
     projected = jnp.einsum("rd,sdc->src", gathered_in, w_qkv, preferred_element_type=jnp.float32)
     projected = (projected + bias_rows[:, None, :]).astype(jnp.bfloat16)
     heads_local = projected.shape[2] // HEAD_DIM
-    head_parts = projected.reshape(3, cells_dev, SLOT, heads_local, HEAD_DIM)
-    attended, log_totals = lax.map(
-        lambda packed: attend_cell(packed[0], packed[1], packed[2], packed[3], block_rows),
-        (head_parts[0], head_parts[1], head_parts[2], live_keys),
-    )
-    attended_low = attended.reshape(group_rows, -1).astype(jnp.bfloat16)
-    attn_sum = lax.psum_scatter(
-        jnp.dot(attended_low, w_out, preferred_element_type=jnp.float32),
-        "tensor",
-        scatter_dimension=0,
-        tiled=True,
-    )
-    middle = inputs + attn_sum + out_bias[0].astype(jnp.float32)
+    head_parts = projected.reshape(3, SLOT, heads_local, HEAD_DIM)
+    attended, log_totals = attend_cell(head_parts[0], head_parts[1], head_parts[2], live_keys, rows)
+    attended_low = attended.astype(jnp.bfloat16)
+
+    def cut(array):
+        return [array[block * rows : (block + 1) * rows] for block in range(4)]
+
+    attn_sum = scatter_relative(
+        cut(jnp.dot(attended_low, w_out, preferred_element_type=jnp.float32))
+    )
+    middle = cells_x.astype(jnp.float32) + attn_sum + out_bias[0].astype(jnp.float32)
     normed_mid, scaled_mid, inverse_mid = normalize(middle, norm_gain[1], norm_shift[1])
-    normed_mid_low = normed_mid.astype(jnp.bfloat16)
-    up_full, bias_full, down_full = (w_up, up_bias, w_down)
-    ffn_rows = lax.all_gather(normed_mid_low, "tensor", axis=0, tiled=True)
-    hidden = jnp.dot(ffn_rows, up_full, preferred_element_type=jnp.float32) + bias_full.astype(
+    ffn_rows = jnp.concatenate(gather_relative(normed_mid.astype(jnp.bfloat16)))
+    hidden = jnp.dot(ffn_rows, w_up, preferred_element_type=jnp.float32) + up_bias.astype(
         jnp.float32
     )
     active, gelu_back = jax.vjp(exact_gelu, hidden)
     active_low = active.astype(jnp.bfloat16)
-    branch = lax.psum_scatter(
-        jnp.dot(active_low, w_down, preferred_element_type=jnp.float32).astype(jnp.bfloat16),
-        "tensor",
-        scatter_dimension=0,
-        tiled=True,
-    ).astype(jnp.float32)
+    hidden_grad = gelu_back(contract_last(grad_rows, w_down))[0].astype(jnp.bfloat16)
+    mid_norm_grad = scatter_relative(cut(contract_last(hidden_grad, w_up)))
+    branch = scatter_relative(cut(jnp.dot(active_low, w_down, preferred_element_type=jnp.float32)))
     output = jnp.where(live_rows[:, None], middle + branch + out_bias[1].astype(jnp.float32), 0.0)
     block_out = output.astype(jnp.bfloat16)
-    out_grad = jnp.where(live_rows[:, None], cotangent, jnp.zeros_like(cotangent))
-    grad_rows = lax.all_gather(out_grad, "tensor", axis=0, tiled=True)
-    hidden_grad = gelu_back(contract_last(grad_rows, down_full))[0].astype(jnp.bfloat16)
     down_grad = contract_first(active_low, grad_rows)
     up_grad = contract_first(ffn_rows, hidden_grad)
     up_bias_grad = jnp.sum(hidden_grad, axis=0, dtype=jnp.float32)
-    mid_norm_grad = lax.psum_scatter(
-        contract_last(hidden_grad, w_up), "tensor", scatter_dimension=0, tiled=True
-    )
     mid_back, gain_mid, shift_mid = normalize_back(
         mid_norm_grad, scaled_mid, inverse_mid, norm_gain[1]
     )
     middle_grad = out_grad.astype(jnp.float32) + mid_back
-    middle_rows = lax.all_gather(middle_grad.astype(jnp.bfloat16), "tensor", axis=0, tiled=True)
+    middle_rows = jnp.concatenate(gather_relative(middle_grad.astype(jnp.bfloat16)))
+    ffn_grads = sum_cells(jnp.concatenate([up_grad, down_grad]))
+    up_grad, down_grad = ffn_grads[: up_grad.shape[0]], ffn_grads[up_grad.shape[0] :]
     attended_grad = contract_last(middle_rows, w_out).astype(jnp.bfloat16)
     out_weight_grad = contract_first(attended_low, middle_rows)
-    grad_heads = attended_grad.reshape(cells_dev, SLOT, heads_local, HEAD_DIM)
-    query_grad, key_grad, value_grad = lax.map(
-        lambda packed: attend_back(
-            packed[0], packed[1], packed[2], packed[3], packed[4], packed[5], block_rows
+    grad_heads = attended_grad.reshape(SLOT, heads_local, HEAD_DIM)
+    query_grad, key_grad, value_grad = attend_back(
+        head_parts[0], head_parts[1], head_parts[2], grad_heads, log_totals, live_keys, rows
+    )
+    qkv_grad = jnp.stack([query_grad, key_grad, value_grad])
+    in_norm_part = jnp.einsum("src,sdc->rd", qkv_grad, w_qkv, preferred_element_type=jnp.float32)
+    in_norm_grad = scatter_relative(cut(in_norm_part))
+    qkv_weight_grad = jnp.einsum(
+        "rd,src->sdc", gathered_in, qkv_grad, preferred_element_type=jnp.float32
+    )
+    query_bias = jnp.sum(qkv_grad[0], axis=0, dtype=jnp.float32)
+    value_bias = jnp.sum(qkv_grad[2], axis=0, dtype=jnp.float32)
+    own = slice(0, rows)
+    in_back, _, _ = normalize_back(in_norm_grad, scaled_in[own], inverse_in[own], norm_gain[0])
+    input_grad = (middle_grad + in_back).astype(jnp.bfloat16)
+    shared = sum_small(
+        jnp.stack(
+            [
+                jnp.sum(in_norm_part * scaled_in, axis=0),
+                gain_mid,
+                jnp.sum(in_norm_part, axis=0),
+                shift_mid,
+                jnp.sum(middle_grad, axis=0),
+                jnp.sum(out_grad, axis=0, dtype=jnp.float32),
+            ]
         ),
-        (head_parts[0], head_parts[1], head_parts[2], grad_heads, log_totals, live_keys),
-    )
-    qkv_grad = jnp.stack([query_grad, key_grad, value_grad]).reshape(3, group_rows, -1)
-    qkv_weight_grad = jnp.einsum(
-        "src,rd->sdc", qkv_grad, gathered_in, preferred_element_type=jnp.float32
-    )
-    qv_bias_grad = jnp.stack(
-        [
-            jnp.sum(qkv_grad[0], axis=0, dtype=jnp.float32),
-            jnp.sum(qkv_grad[2], axis=0, dtype=jnp.float32),
-        ]
-    )
-    in_norm_grad = lax.psum_scatter(
-        jnp.einsum("src,sdc->rd", qkv_grad, w_qkv, preferred_element_type=jnp.float32),
-        "tensor",
-        scatter_dimension=0,
-        tiled=True,
-    )
-    in_back, gain_in, shift_in = normalize_back(in_norm_grad, scaled_in, inverse_in, norm_gain[0])
-    input_grad = (middle_grad + in_back).astype(jnp.bfloat16)
-    gain_grad, shift_grad, bias_grad = lax.psum(
-        (
-            jnp.stack([gain_in, gain_mid]),
-            jnp.stack([shift_in, shift_mid]),
-            jnp.stack([jnp.sum(middle_grad, axis=0), jnp.sum(out_grad, axis=0, dtype=jnp.float32)]),
-        ),
-        "tensor",
-    )
-    (
-        qkv_weight_grad,
-        qv_bias_grad,
-        out_weight_grad,
-        up_grad,
-        up_bias_grad,
-        down_grad,
-        gain_grad,
-        shift_grad,
-        bias_grad,
-    ) = lax.psum(
-        (
-            qkv_weight_grad,
-            qv_bias_grad,
-            out_weight_grad,
-            up_grad,
-            up_bias_grad,
-            down_grad,
-            gain_grad,
-            shift_grad,
-            bias_grad,
-        ),
-        "dp",
-    )
+        ("tensor", "dp"),
+    )
+    sharded = sum_small(jnp.concatenate([up_bias_grad, query_bias, value_bias])[None], ("dp",))[0]
+    columns = w_qkv.shape[2]
+    attn_grads = sum_cells(
+        jnp.concatenate([out_weight_grad, qkv_weight_grad.reshape(-1, width)])
+    )
+    out_weight_grad = attn_grads[:columns]
+    qkv_weight_grad = attn_grads[columns:].reshape(w_qkv.shape)
+    units = up_bias.shape[0]
     return (
         block_out,
         input_grad,
-        gain_grad,
-        shift_grad,
-        bias_grad,
+        shared[0:2],
+        shared[2:4],
+        shared[4:6],
         qkv_weight_grad,
-        qv_bias_grad,
+        sharded[units:].reshape(2, columns),
         out_weight_grad,
         up_grad,
-        up_bias_grad,
+        sharded[:units],
         down_grad,
     )
 

time: 842 us -> 534 us (0.63)
  waiting for transfers between devices: 469 us -> 160 us
  blocking collectives: 50.4 us -> 0 us
  starting transfers between devices: 0.76 us -> 45.2 us
  between operations: 15.4 us -> 3.12 us
  local copies, waits for them, and re-layouts: 33 us -> 43.8 us
    psum x1 -> x0, waiting for transfers between devices: 182 us -> none  [per_device(): lax.psum((qkv_weight_grad, qv_bias_grad, out_weight_grad, up_grad, up_bia...]
    reduce_scatter x4 -> x0, waiting for transfers between devices: 181 us -> none  [the longest x1 57.7 us: per_device(): lax.psum_scatter(jnp.dot(attended_low, w_out, preferred_element_type=jnp....]
    ppermute x0 -> x56, waiting for transfers between devices: none -> 160 us  [pair_swap(): lax.ppermute(array, axis, [(source, source ^ bit) for source in range(siz...]
    all_gather x4 -> x0, waiting for transfers between devices: 105 us -> none  [the longest x1 29.9 us: per_device(): lax.all_gather(normed_in.astype(jnp.bfloat16), 'tensor', axis=0, tiled=True)]
    psum x2 -> x0, blocking collectives: 50.4 us -> none  [the longest x1 40.2 us: per_device(): lax.psum((qkv_weight_grad, qv_bias_grad, out_weight_grad, up_grad, up_bia...]
    ppermute x0 -> x56, starting transfers between devices: none -> 45.2 us  [pair_swap(): lax.ppermute(array, axis, [(source, source ^ bit) for source in range(siz...]
    dot_general x1 -> x2, matrix products: 7.49 us -> 25.1 us  [the longest x1 21 us: per_device(): jnp.dot(ffn_rows, w_up, preferred_element_type=jnp.float32)]
    dot_general x3, matrix products: 28.7 us -> 16.9 us  [contract_last(): lax.dot_general(left, right, (((1,), (1,)), ((), ())), preferred_element_...]
  transfers between devices with their start and end apart: 9 -> 56, of which waited for: 9 -> 28; matrix products, arithmetic and copies ran while one was open for 6% -> 20% of each run, Pallas kernels for 0% -> 0%
where the time goes in v1:
time: 534 us; the launch traced here: 525 us
  matrix products  178 us (33%)
  waiting for transfers between devices  160 us (30%)
  other arithmetic  81.6 us (15%)
  starting transfers between devices  45.2 us (8%)
  local copies, waits for them, and re-layouts  43.8 us (8%)
  loops' own time  13.9 us (3%)
    ppermute x56, waiting for transfers between devices, pair_swap(): lax.ppermute(array, axis, [(source, source ^ bit) for source in range(siz...  160 us
    ppermute x56, starting transfers between devices, pair_swap(): lax.ppermute(array, axis, [(source, source ^ bit) for source in range(siz...  45.2 us
    dot_general x4, matrix products, one_block(): jnp.einsum('hqk,khe->qhe', score_grad, key_heads, preferred_element_type=...  22.6 us
    dot_general x4, matrix products, one_block(): jnp.einsum('hqk,qhe->khe', soft_low, block_grads, preferred_element_type=...  21.5 us
    convert_element_type x4, other arithmetic, one_block(): (score_scale * softmaxed * (prob_grad - row_inner)).astype(jnp.bfloat16)  21.3 us
    dot_general x1, matrix products, per_device(): jnp.dot(ffn_rows, w_up, preferred_element_type=jnp.float32)  21 us
    dot_general x4, matrix products, one_block(): jnp.einsum('qhe,khe->hqk', block_grads, value_heads, preferred_element_ty...  19.4 us
    dot_general x8, matrix products, masked_scores(): jnp.einsum('qhe,khe->hqk', block_queries, key_heads, preferred_element_ty...  19 us
  transfers between devices with their start and end apart: 56, of which 28 were waited for; matrix products, arithmetic and copies ran while one was open for 20% of the time, Pallas kernels for 0%

profile of v1, /device:TPU:0, one launch (start us, length us, event | category | flops | bytes accessed | tf_op | source)
XLA Modules:
  0.0 525.5 jit_solution(3960700612700514884)
XLA Ops:
  5.8 15.7 %collective-permute-done.1 = bf16[512,768]{1,0:T(8,128)(2,1)S(1)} collective-permute-done((bf16[512,768]{1,0:T(8,128)(2,1)}, bf16[512,768]{1,0:T(8,128)(2,1)S(1)}, u32[]{:S(2)}, u32[]{:S(2)}) %collective-permute-start.1) | collective-permute-done | bytes 786464 | tf_op jit(solution)/shard_map/ppermute | solution.py:120
  35.0 42.8 %while.27 = (s32[]{:T(128)}, bf16[4,512,3,64]{1,3,2,0:T(8,128)(2,1)}, f32[4,3,512]{2,1,0:T(4,128)}, pred[2048]{0:T(1024)(128)(4,1)S(1)}, s32[4]{0:T(128)S(1)}, /...) while((s32[]{:T(128)}, ...), condition=%wide.region_6.7_spmd, body=%wide.region_3.6_spmd.sunk | while | flops 843053568 | bytes 46264568 | solution.py:75
  86.6 17.5 %collective-permute-done.5 = bf16[512,768]{1,0:T(8,128)(2,1)S(1)} collective-permute-done((bf16[512,768]{1,0:T(8,128)(2,1)S(1)}, bf16[512,768]{1,0:T(8,128)(2,1)S(1)}, u32[]{:S(2)}, u32[]{:S(2)}) %collective-permute-start.5) | collective-permute-done | bytes 786464 | tf_op jit(solution)/shard_map/ppermute | solution.py:120
  109.8 17.0 %collective-permute-done.7 = bf16[512,768]{1,0:T(8,128)(2,1)} collective-permute-done((bf16[512,768]{1,0:T(8,128)(2,1)}, bf16[512,768]{1,0:T(8,128)(2,1)}, u32[]{:S(2)}, u32[]{:S(2)}) %collective-permute-start.7) | collective-permute-done | bytes 786464 | tf_op jit(solution)/shard_map/ppermute | solution.py:120
  128.6 13.6 %collective-permute-done.13 = bf16[512,768]{1,0:T(8,128)(2,1)} collective-permute-done((bf16[512,768]{1,0:T(8,128)(2,1)}, bf16[512,768]{1,0:T(8,128)(2,1)}, u32[]{:S(2)}, u32[]{:S(2)}) %collective-permute-start.13) | collective-permute-done | bytes 786464 | tf_op jit(solution)/shard_map/ppermute | solution.py:120
  142.2 21.0 %multiply_convert_fusion.1 = (bf16[2048,768]{1,0:T(8,128)(2,1)S(1)}, f32[2048,768]{1,0:T(8,128)}, f32[2048,768]{1,0:T(8,128)}) fusion(f32[768]{0:T(1024)} %convert_element_type.296, bf16[768,768]{1,0:T(8,128)(2,1)S(1)} %copy-done, bf16[512,768]{1,0:T(8,128)(2,1)} %collective-permute-done.8, bf16[512,768]{1,0:T(8,128)(2,1)} %collective-permute-done.7, ...), kind=kOutput, calls=%fused_computation.49 | convolution fusion | flops 2532311040 | bytes 20057088 | tf_op jit(solution)/shard_map/dot_general | solution.py:222
  173.0 10.3 %convert_reduce_fusion.1 = (f32[768]{0:T(1024)}, bf16[2048,768]{1,0:T(8,128)(2,1)S(1)}) fusion(f32[2048,768]{1,0:T(8,128)} %get-tuple-element.237, bf16[768,768]{1,0:T(8,128)(2,1)S(1)} %copy-done.52, bf16[512,768]{1,0:T(8,128)(2,1)S(1)} %collective-permute-done.14, bf16[512,768]{1,0:T(8,128)(2,1)} %collective-permute-done.13, ...), kind=kOutput, calls=%fused_computation.46 | convolution fusion | flops 2455239936 | bytes 20060160 | tf_op jit(solution)/shard_map/dot_general | solution.py:39
  183.3 5.6 %fusion.75 = f32[768,768]{1,0:T(8,128)S(1)} fusion(bf16[2048,768]{1,0:T(8,128)(2,1)S(1)} %get-tuple-element.272, bf16[512,768]{1,0:T(8,128)(2,1)} %collective-permute-done.8, bf16[512,768]{1,0:T(8,128)(2,1)} %collective-permute-done.7, bf16[512,768]{1,0:T(8,128)(2,1)} %collective-permute-done.6, bf16[512,768]{1,0:T(8,128)(2,1)} %add_convert_fusion.4), kind=kOutput, calls=%fused_computation.144 | convolution fusion | flops 2428502016 | bytes 8650752 | tf_op jit(solution)/shard_map/dot_general | solution.py:45
  195.8 8.7 %collective-permute-done.44 = bf16[384,768]{1,0:T(8,128)(2,1)S(1)} collective-permute-done((bf16[384,768]{1,0:T(8,128)(2,1)S(1)}, bf16[384,768]{1,0:T(8,128)(2,1)S(1)}, u32[]{:S(2)}, u32[]{:S(2)}) %collective-permute-start.44) | collective-permute-done | bytes 589856 | tf_op jit(solution)/shard_map/ppermute | solution.py:120
  209.7 11.8 %collective-permute-done.45 = bf16[192,768]{1,0:T(8,128)(2,1)S(1)} collective-permute-done((bf16[192,768]{1,0:T(8,128)(2,1)S(1)}, bf16[192,768]{1,0:T(8,128)(2,1)S(1)}, u32[]{:S(2)}, u32[]{:S(2)}) %collective-permute-start.45) | collective-permute-done | bytes 294944 | tf_op jit(solution)/shard_map/ppermute | solution.py:120
  223.3 7.1 %collective-permute-done.46 = bf16[96,768]{1,0:T(8,128)(2,1)S(1)} collective-permute-done((bf16[96,768]{1,0:T(8,128)(2,1)S(1)}, bf16[96,768]{1,0:T(8,128)(2,1)S(1)}, u32[]{:S(2)}, u32[]{:S(2)}) %collective-permute-start.46) | collective-permute-done | bytes 147488 | tf_op jit(solution)/shard_map/ppermute | solution.py:120
  234.1 9.1 %collective-permute-done.17 = bf16[512,768]{1,0:T(8,128)(2,1)S(1)} collective-permute-done((bf16[512,768]{1,0:T(8,128)(2,1)S(1)}, bf16[512,768]{1,0:T(8,128)(2,1)S(1)}, u32[]{:S(2)}, u32[]{:S(2)}) %collective-permute-start.17) | collective-permute-done | bytes 786464 | tf_op jit(solution)/shard_map/ppermute | solution.py:120
  257.6 5.6 %collective-permute-done.48 = bf16[192,768]{1,0:T(8,128)(2,1)S(1)} collective-permute-done((bf16[192,768]{1,0:T(8,128)(2,1)S(1)}, bf16[192,768]{1,0:T(8,128)(2,1)S(1)}, u32[]{:S(2)}, u32[]{:S(2)}) %collective-permute-start.48) | collective-permute-done | bytes 294944 | tf_op jit(solution)/shard_map/ppermute | solution.py:120
  276.3 7.9 %collective-permute-done.55 = bf16[384,768]{1,0:T(8,128)(2,1)} collective-permute-done((bf16[384,768]{1,0:T(8,128)(2,1)S(1)}, bf16[384,768]{1,0:T(8,128)(2,1)}, u32[]{:S(2)}, u32[]{:S(2)}) %collective-permute-start.55) | collective-permute-done | bytes 589856 | tf_op jit(solution)/shard_map/ppermute | solution.py:120
  292.1 121.4 %while.28 = (s32[]{:T(128)}, f32[2048,3,64]{0,2,1:T(8,128)S(1)}, f32[2048,3,64]{0,2,1:T(8,128)}, bf16[4,512,3,64]{1,3,2,0:T(8,128)(2,1)}, s32[4]{0:T(128)S(1)}, ...) while((s32[]{:T(128)}, f32[2048,3,64]{0,2,1:T(8,128)S(1)}, ...), condition=%wide.region_13.14_spmd.clone, body=%wide.region_11.13_spmd.clone.sunk | while | flops 2065168896 | bytes 129417528 | solution.py:108
  308.7 5.3 %multiply_convert_fusion.3 = bf16[3,512,2048]{2,1,0:T(8,128)(2,1)} fusion(f32[3,512,2048]{2,1,0:T(8,128)S(1)} %get-tuple-element.401, f32[3,512,2048]{2,1,0:T(8,128)S(1)} %fusion.160, f32[3,512]{1,0:T(4,128)S(1)} %get-tuple-element.402, f32[3,512]{1,0:T(4,128)S(1)} %dynamic-slice_bitcast_fusion.2, pred[2048]{0:T(1024)(128)(4,1)S(1)} %get-tuple-element.477), kind=kLoop, calls=%fused_computation.14.clone.1 | loop fusion | flops 22020096 | bytes 31471616 | tf_op jit(solution)/shard_map/while/body/eval_jaxpr/convert_element_type | solution.py:95
  314.0 5.6 %fusion.163 = bf16[4,512,3,64]{1,3,2,0:T(8,128)(2,1)} fusion(bf16[4,512,3,64]{1,3,2,0:T(8,128)(2,1)} %get-tuple-element.458, s32[]{:T(128)S(6)} %copy.48, bf16[3,512,2048]{2,1,0:T(8,128)(2,1)} %multiply_convert_fusion.3, bf16[2048,3,64]{0,2,1:T(8,128)(2,1)S(1)} %get-tuple-element.478), kind=kOutput, calls=%fused_computation.25.clone.1 | convolution fusion | flops 402653184 | bytes 7471108 | tf_op jit(solution)/shard_map/while/body/eval_jaxpr/hqk,khe->qhe/dot_general | solution.py:96
  328.7 5.5 %fusion.162 = f32[2048,3,64]{0,2,1:T(8,128)} fusion(f32[3,512,2048]{2,1,0:T(8,128)S(1)} %fusion.160, f32[3,512]{1,0:T(4,128)S(1)} %dynamic-slice_bitcast_fusion.2, pred[2048]{0:T(1024)(128)(4,1)S(1)} %get-tuple-element.477, f32[2048,3,64]{0,2,1:T(8,128)} %get-tuple-element.457, pred[]{:T(512)S(6)} %compare.11, ...), kind=kOutput, calls=%fused_computation.23.clone.1 | convolution fusion | flops 416022528 | bytes 15933445 | tf_op jit(solution)/shard_map/while/body/eval_jaxpr/hqk,qhe->khe/dot_general | solution.py:102
  344.4 5.6 %fusion.163 = bf16[4,512,3,64]{1,3,2,0:T(8,128)(2,1)} fusion(bf16[4,512,3,64]{1,3,2,0:T(8,128)(2,1)} %get-tuple-element.458, s32[]{:T(128)S(6)} %copy.48, bf16[3,512,2048]{2,1,0:T(8,128)(2,1)} %multiply_convert_fusion.3, bf16[2048,3,64]{0,2,1:T(8,128)(2,1)S(1)} %get-tuple-element.478), kind=kOutput, calls=%fused_computation.25.clone.1 | convolution fusion | flops 402653184 | bytes 7471108 | tf_op jit(solution)/shard_map/while/body/eval_jaxpr/hqk,khe->qhe/dot_general | solution.py:96
  359.1 5.5 %fusion.162 = f32[2048,3,64]{0,2,1:T(8,128)} fusion(f32[3,512,2048]{2,1,0:T(8,128)S(1)} %fusion.160, f32[3,512]{1,0:T(4,128)S(1)} %dynamic-slice_bitcast_fusion.2, pred[2048]{0:T(1024)(128)(4,1)S(1)} %get-tuple-element.477, f32[2048,3,64]{0,2,1:T(8,128)} %get-tuple-element.457, pred[]{:T(512)S(6)} %compare.11, ...), kind=kOutput, calls=%fused_computation.23.clone.1 | convolution fusion | flops 416022528 | bytes 15933445 | tf_op jit(solution)/shard_map/while/body/eval_jaxpr/hqk,qhe->khe/dot_general | solution.py:102
  374.8 5.6 %fusion.163 = bf16[4,512,3,64]{1,3,2,0:T(8,128)(2,1)} fusion(bf16[4,512,3,64]{1,3,2,0:T(8,128)(2,1)} %get-tuple-element.458, s32[]{:T(128)S(6)} %copy.48, bf16[3,512,2048]{2,1,0:T(8,128)(2,1)} %multiply_convert_fusion.3, bf16[2048,3,64]{0,2,1:T(8,128)(2,1)S(1)} %get-tuple-element.478), kind=kOutput, calls=%fused_computation.25.clone.1 | convolution fusion | flops 402653184 | bytes 7471108 | tf_op jit(solution)/shard_map/while/body/eval_jaxpr/hqk,khe->qhe/dot_general | solution.py:96
  389.5 5.5 %fusion.162 = f32[2048,3,64]{0,2,1:T(8,128)} fusion(f32[3,512,2048]{2,1,0:T(8,128)S(1)} %fusion.160, f32[3,512]{1,0:T(4,128)S(1)} %dynamic-slice_bitcast_fusion.2, pred[2048]{0:T(1024)(128)(4,1)S(1)} %get-tuple-element.477, f32[2048,3,64]{0,2,1:T(8,128)} %get-tuple-element.457, pred[]{:T(512)S(6)} %compare.11, ...), kind=kOutput, calls=%fused_computation.23.clone.1 | convolution fusion | flops 416022528 | bytes 15933445 | tf_op jit(solution)/shard_map/while/body/eval_jaxpr/hqk,qhe->khe/dot_general | solution.py:102
  405.2 5.6 %fusion.163 = bf16[4,512,3,64]{1,3,2,0:T(8,128)(2,1)} fusion(bf16[4,512,3,64]{1,3,2,0:T(8,128)(2,1)} %get-tuple-element.458, s32[]{:T(128)S(6)} %copy.48, bf16[3,512,2048]{2,1,0:T(8,128)(2,1)} %multiply_convert_fusion.3, bf16[2048,3,64]{0,2,1:T(8,128)(2,1)S(1)} %get-tuple-element.478), kind=kOutput, calls=%fused_computation.25.clone.1 | convolution fusion | flops 402653184 | bytes 7471108 | tf_op jit(solution)/shard_map/while/body/eval_jaxpr/hqk,khe->qhe/dot_general | solution.py:96
  438.9 10.1 %fusion.89 = (f32[768]{0:T(1024)S(1)}, f32[768]{0:T(1024)S(1)}, bf16[2048,768]{1,0:T(8,128)(2,1)}, f32[2048,768]{1,0:T(8,128)}, f32[2048,768]{1,0:T(8,128)}) fusion(f32[2048]{0:T(1024)S(1)} %copy-done.40, f32[2048]{0:T(1024)S(1)} %copy-done.31, bf16[512,768]{1,0:T(8,128)(2,1)} %copy-done.22, bf16[512,768]{1,0:T(8,128)(2,1)} %copy-done.18, ...), kind=kOutput, calls=%fused_computation.197 | convolution fusion | flops 1836317184 | bytes 22140928 | tf_op jit(solution)/shard_map/src,sdc->rd/dot_general | solution.py:249
  (409 shorter events, 303.0 us)
Async XLA Ops:
  0.7 20.8 %collective-permute-start.1 = (bf16[512,768]{1,0:T(8,128)(2,1)}, bf16[512,768]{1,0:T(8,128)(2,1)S(1)}, u32[]{:S(2)}, u32[]{:S(2)}) collective-permute-start(bf16[512,768]{1,0:T(8,128)(2,1)} %param.17), channel_id=1, source_target_pairs={{0,2},{1,3},{2,0},{3,1},{4,6},{5,7},{6,4},{7,5},{8,10},{9,11},{10,... | collective-permute-start | bytes 2359304 | tf_op jit(solution)/shard_map/ppermute | solution.py:120
  3.7 20.7 %collective-permute-start = (bf16[512,768]{1,0:T(8,128)(2,1)}, bf16[512,768]{1,0:T(8,128)(2,1)S(1)}, u32[]{:S(2)}, u32[]{:S(2)}) collective-permute-start(bf16[512,768]{1,0:T(8,128)(2,1)} %param.17), channel_id=1, source_target_pairs={{0,1},{1,0},{2,3},{3,2},{4,5},{5,4},{6,7},{7,6},{8,9},{9,8},{10,11... | collective-permute-start | bytes 2359304 | tf_op jit(solution)/shard_map/ppermute | solution.py:120
  84.1 19.9 %collective-permute-start.5 = (bf16[512,768]{1,0:T(8,128)(2,1)S(1)}, bf16[512,768]{1,0:T(8,128)(2,1)S(1)}, u32[]{:S(2)}, u32[]{:S(2)}) collective-permute-start(bf16[512,768]{1,0:T(8,128)(2,1)S(1)} %fusion.57), channel_id=1, source_target_pairs={{0,2},{1,3},{2,0},{3,1},{4,6},{5,7},{6,4},{7,5},{8,10},{9,11},{10,... | collective-permute-start | bytes 2359304 | tf_op jit(solution)/shard_map/ppermute | solution.py:120
  106.0 20.7 %collective-permute-start.7 = (bf16[512,768]{1,0:T(8,128)(2,1)}, bf16[512,768]{1,0:T(8,128)(2,1)}, u32[]{:S(2)}, u32[]{:S(2)}) collective-permute-start(bf16[512,768]{1,0:T(8,128)(2,1)} %add_convert_fusion.4), channel_id=1, source_target_pairs={{0,2},{1,3},{2,0},{3,1},{4,6},{5,7},{6,4},{7,5},{8,10},{9,11},{10,... | collective-permute-start | bytes 2359304 | tf_op jit(solution)/shard_map/ppermute | solution.py:120
  109.5 32.7 %collective-permute-start.13 = (bf16[512,768]{1,0:T(8,128)(2,1)}, bf16[512,768]{1,0:T(8,128)(2,1)}, u32[]{:S(2)}, u32[]{:S(2)}) collective-permute-start(bf16[512,768]{1,0:T(8,128)(2,1)} %get-tuple-element.231), channel_id=1, source_target_pairs={{0,2},{1,3},{2,0},{3,1},{4,6},{5,7},{6,4},{7,5},{8,10},{9,11},{10,... | collective-permute-start | bytes 2359304 | tf_op jit(solution)/shard_map/ppermute | solution.py:120
  109.8 32.4 %collective-permute-start.6 = (bf16[512,768]{1,0:T(8,128)(2,1)}, bf16[512,768]{1,0:T(8,128)(2,1)}, u32[]{:S(2)}, u32[]{:S(2)}) collective-permute-start(bf16[512,768]{1,0:T(8,128)(2,1)} %add_convert_fusion.4), channel_id=1, source_target_pairs={{0,1},{1,0},{2,3},{3,2},{4,5},{5,4},{6,7},{7,6},{8,9},{9,8},{10,11... | collective-permute-start | bytes 2359304 | tf_op jit(solution)/shard_map/ppermute | solution.py:120
  126.8 36.4 %collective-permute-start.12 = (bf16[512,768]{1,0:T(8,128)(2,1)}, bf16[512,768]{1,0:T(8,128)(2,1)}, u32[]{:S(2)}, u32[]{:S(2)}) collective-permute-start(bf16[512,768]{1,0:T(8,128)(2,1)} %get-tuple-element.231), channel_id=1, source_target_pairs={{0,1},{1,0},{2,3},{3,2},{4,5},{5,4},{6,7},{7,6},{8,9},{9,8},{10,11... | collective-permute-start | bytes 2359304 | tf_op jit(solution)/shard_map/ppermute | solution.py:120
  142.2 21.0 %collective-permute-start.14 = (bf16[512,768]{1,0:T(8,128)(2,1)}, bf16[512,768]{1,0:T(8,128)(2,1)S(1)}, u32[]{:S(2)}, u32[]{:S(2)}) collective-permute-start(bf16[512,768]{1,0:T(8,128)(2,1)} %collective-permute-done.13), channel_id=1, source_target_pairs={{0,1},{1,0},{2,3},{3,2},{4,5},{5,4},{6,7},{7,6},{8,9},{9,8},{10,11... | collective-permute-start | bytes 2359304 | tf_op jit(solution)/shard_map/ppermute | solution.py:120
  168.6 25.6 %collective-permute-start.50 = (bf16[384,768]{1,0:T(8,128)(2,1)}, bf16[384,768]{1,0:T(8,128)(2,1)}, u32[]{:S(2)}, u32[]{:S(2)}) collective-permute-start(bf16[384,768]{1,0:T(8,128)(2,1)} %dynamic-slice_convert_fusion), channel_id=1, source_target_pairs={{0,8},{4,12},{8,0},{12,4},{16,24},{20,28},{24,16},{28,20},{1,9},{5... | collective-permute-start | bytes 1769480 | tf_op jit(solution)/shard_map/ppermute | solution.py:120
  190.6 54.0 %collective-permute-start.9 = (bf16[512,768]{1,0:T(8,128)(2,1)S(1)}, bf16[512,768]{1,0:T(8,128)(2,1)S(1)}, u32[]{:S(2)}, u32[]{:S(2)}) collective-permute-start(bf16[512,768]{1,0:T(8,128)(2,1)S(1)} %get-tuple-element.250), channel_id=1, source_target_pairs={{0,1},{1,0},{2,3},{3,2},{4,5},{5,4},{6,7},{7,6},{8,9},{9,8},{10,11... | collective-permute-start | bytes 2359304 | tf_op jit(solution)/shard_map/ppermute | solution.py:120
  194.0 40.0 %collective-permute-start.15 = (bf16[512,768]{1,0:T(8,128)(2,1)S(1)}, bf16[512,768]{1,0:T(8,128)(2,1)S(1)}, u32[]{:S(2)}, u32[]{:S(2)}) collective-permute-start(bf16[512,768]{1,0:T(8,128)(2,1)S(1)} %get-tuple-element.248), channel_id=1, source_target_pairs={{0,1},{1,0},{2,3},{3,2},{4,5},{5,4},{6,7},{7,6},{8,9},{9,8},{10,11... | collective-permute-start | bytes 2359304 | tf_op jit(solution)/shard_map/ppermute | solution.py:120
  204.5 18.7 %collective-permute-start.51 = (bf16[192,768]{1,0:T(8,128)(2,1)S(1)}, bf16[192,768]{1,0:T(8,128)(2,1)S(1)}, u32[]{:S(2)}, u32[]{:S(2)}) collective-permute-start(bf16[192,768]{1,0:T(8,128)(2,1)S(1)} %dynamic-slice_convert_fusion.2), channel_id=1, source_target_pairs={{0,16},{4,20},{8,24},{12,28},{16,0},{20,4},{24,8},{28,12},{1,17},{... | collective-permute-start | bytes 884744 | tf_op jit(solution)/shard_map/ppermute | solution.py:120
  208.0 36.7 %collective-permute-start.11 = (bf16[512,768]{1,0:T(8,128)(2,1)S(1)}, bf16[512,768]{1,0:T(8,128)(2,1)S(1)}, u32[]{:S(2)}, u32[]{:S(2)}) collective-permute-start(bf16[512,768]{1,0:T(8,128)(2,1)S(1)} %fusion.51), channel_id=1, source_target_pairs={{0,2},{1,3},{2,0},{3,1},{4,6},{5,7},{6,4},{7,5},{8,10},{9,11},{10,... | collective-permute-start | bytes 2359304 | tf_op jit(solution)/shard_map/ppermute | solution.py:120
  221.6 21.6 %collective-permute-start.17 = (bf16[512,768]{1,0:T(8,128)(2,1)S(1)}, bf16[512,768]{1,0:T(8,128)(2,1)S(1)}, u32[]{:S(2)}, u32[]{:S(2)}) collective-permute-start(bf16[512,768]{1,0:T(8,128)(2,1)S(1)} %fusion.49), channel_id=1, source_target_pairs={{0,2},{1,3},{2,0},{3,1},{4,6},{5,7},{6,4},{7,5},{8,10},{9,11},{10,... | collective-permute-start | bytes 2359304 | tf_op jit(solution)/shard_map/ppermute | solution.py:120
  230.5 21.4 %collective-permute-start.52 = (bf16[96,768]{1,0:T(8,128)(2,1)S(1)}, bf16[96,768]{1,0:T(8,128)(2,1)S(1)}, u32[]{:S(2)}, u32[]{:S(2)}) collective-permute-start(bf16[96,768]{1,0:T(8,128)(2,1)S(1)} %dynamic-slice_convert_fusion.5), channel_id=1, source_target_pairs={{0,4},{4,0},{8,12},{12,8},{16,20},{20,16},{24,28},{28,24},{1,5},{5... | collective-permute-start | bytes 442376 | tf_op jit(solution)/shard_map/ppermute | solution.py:120
  234.0 19.5 %collective-permute-start.47 = (bf16[96,768]{1,0:T(8,128)(2,1)S(1)}, bf16[96,768]{1,0:T(8,128)(2,1)S(1)}, u32[]{:S(2)}, u32[]{:S(2)}) collective-permute-start(bf16[96,768]{1,0:T(8,128)(2,1)S(1)} %add_convert_fusion.8), channel_id=1, source_target_pairs={{0,16},{4,20},{8,24},{12,28},{16,0},{20,4},{24,8},{28,12},{1,17},{... | collective-permute-start | bytes 442376 | tf_op jit(solution)/shard_map/ppermute | solution.py:120
  263.5 23.6 %collective-permute-start.18 = (bf16[512,768]{1,0:T(8,128)(2,1)}, bf16[512,768]{1,0:T(8,128)(2,1)}, u32[]{:S(2)}, u32[]{:S(2)}) collective-permute-start(bf16[512,768]{1,0:T(8,128)(2,1)} %convert_element_type.309), channel_id=1, source_target_pairs={{0,1},{1,0},{2,3},{3,2},{4,5},{5,4},{6,7},{7,6},{8,9},{9,8},{10,11... | collective-permute-start | bytes 2359304 | tf_op jit(solution)/shard_map/ppermute | solution.py:120
  268.1 19.0 %collective-permute-start.20 = (bf16[512,768]{1,0:T(8,128)(2,1)}, bf16[512,768]{1,0:T(8,128)(2,1)}, u32[]{:S(2)}, u32[]{:S(2)}) collective-permute-start(bf16[512,768]{1,0:T(8,128)(2,1)} %collective-permute-done.19), channel_id=1, source_target_pairs={{0,1},{1,0},{2,3},{3,2},{4,5},{5,4},{6,7},{7,6},{8,9},{9,8},{10,11... | collective-permute-start | bytes 2359304 | tf_op jit(solution)/shard_map/ppermute | solution.py:120
  429.5 22.7 %collective-permute-start.41 = (f32[1,1152]{1,0:T(1,128)S(1)}, f32[1,1152]{1,0:T(1,128)S(1)}, u32[]{:S(2)}, u32[]{:S(2)}) collective-permute-start(f32[1,1152]{1,0:T(1,128)S(1)} %broadcast_in_dim.94), channel_id=1, source_target_pairs={{0,4},{4,0},{8,12},{12,8},{16,20},{20,16},{24,28},{28,24},{1,5},{5... | collective-permute-start | bytes 13832 | tf_op jit(solution)/shard_map/ppermute | solution.py:120
  434.9 38.4 %collective-permute-start.35 = (bf16[192,768]{1,0:T(8,128)(2,1)}, bf16[192,768]{1,0:T(8,128)(2,1)}, u32[]{:S(2)}, u32[]{:S(2)}) collective-permute-start(bf16[192,768]{1,0:T(8,128)(2,1)} %dynamic-slice_convert_fusion.4), channel_id=1, source_target_pairs={{0,8},{4,12},{8,0},{12,4},{16,24},{20,28},{24,16},{28,20},{1,9},{5... | collective-permute-start | bytes 884744 | tf_op jit(solution)/shard_map/ppermute | solution.py:120
  455.2 19.6 %collective-permute-start.29 = (bf16[192,768]{1,0:T(8,128)(2,1)}, bf16[192,768]{1,0:T(8,128)(2,1)S(1)}, u32[]{:S(2)}, u32[]{:S(2)}) collective-permute-start(bf16[192,768]{1,0:T(8,128)(2,1)} %fusion.68), channel_id=1, source_target_pairs={{0,4},{4,0},{8,12},{12,8},{16,20},{20,16},{24,28},{28,24},{1,5},{5... | collective-permute-start | bytes 884744 | tf_op jit(solution)/shard_map/ppermute | solution.py:120
  458.9 60.4 %collective-permute-start.21 = (bf16[512,768]{1,0:T(8,128)(2,1)}, bf16[512,768]{1,0:T(8,128)(2,1)}, u32[]{:S(2)}, u32[]{:S(2)}) collective-permute-start(bf16[512,768]{1,0:T(8,128)(2,1)} %get-tuple-element.246), channel_id=1, source_target_pairs={{0,1},{1,0},{2,3},{3,2},{4,5},{5,4},{6,7},{7,6},{8,9},{9,8},{10,11... | collective-permute-start | bytes 2359304 | tf_op jit(solution)/shard_map/ppermute | solution.py:120
  460.4 37.3 %collective-permute-start.22 = (bf16[512,768]{1,0:T(8,128)(2,1)}, bf16[512,768]{1,0:T(8,128)(2,1)}, u32[]{:S(2)}, u32[]{:S(2)}) collective-permute-start(bf16[512,768]{1,0:T(8,128)(2,1)} %get-tuple-element.247), channel_id=1, source_target_pairs={{0,1},{1,0},{2,3},{3,2},{4,5},{5,4},{6,7},{7,6},{8,9},{9,8},{10,11... | collective-permute-start | bytes 2359304 | tf_op jit(solution)/shard_map/ppermute | solution.py:120
  499.5 19.8 %collective-permute-start.23 = (bf16[512,768]{1,0:T(8,128)(2,1)S(1)}, bf16[512,768]{1,0:T(8,128)(2,1)S(1)}, u32[]{:S(2)}, u32[]{:S(2)}) collective-permute-start(bf16[512,768]{1,0:T(8,128)(2,1)S(1)} %fusion.46), channel_id=1, source_target_pairs={{0,2},{1,3},{2,0},{3,1},{4,6},{5,7},{6,4},{7,5},{8,10},{9,11},{10,... | collective-permute-start | bytes 2359304 | tf_op jit(solution)/shard_map/ppermute | solution.py:120
  (99 other events, 840.0 us)
